TPU v7x, 128 devices: a whole 4x4x4 slice. The times are simulated.
128 devices in a mesh: dp: 4 (over y_lo, core), seq: 32 (over x, y_hi, z).
Axes of the slice: x: 4, y: 4 (y_hi: 2, y_lo: 2; y = y_hi * 2 + y_lo), z: 4, core: 2. Of those that a mesh axis runs over, the one named last changes fastest.
Arguments:
- tokens: bfloat16 [4, 16384, 2048], P('dp', 'seq'), may hold values from -5 to 5, as said below
- gain_first: float32 [2048], replicated, may hold values from 0.25 to 1.75
- inputs_first: bfloat16 [2048, 3072], P(('dp', 'seq')), may hold values from -1 to 1, as said below
- output_first: bfloat16 [1024, 2048], P(('dp', 'seq')), may hold values from -0.5 to 0.5
- gain_second: float32 [2048], replicated, may hold values from 0.25 to 1.75
- inputs_second: bfloat16 [2048, 3072], P(('dp', 'seq')), may hold values from -1 to 1, as said below
- output_second: bfloat16 [1024, 2048], P(('dp', 'seq')), may hold values from -0.5 to 0.5
- starts: int32 [4, 32], P('dp'), may hold values from 0 to 32256, as said below
- band_edges: int32 [2], replicated, may hold values from 4 to 62, as said below
Outputs:
- layer_out: bfloat16 [4, 16384, 2048], P('dp', 'seq')
Inputs may be any that keep to these rules, and one draw needn't show every extreme that they name: `tokens`: entries are real-valued and lie within -5 to 5. `inputs_first`: entries lie within -6 / sqrt(2048) to 6 / sqrt(2048). `inputs_second`: entries lie within -6 / sqrt(2048) to 6 / sqrt(2048). `starts`: along a sequence each start exceeds the one before by 512 to 1024; the first is at most 512. band_edges[0] < band_edges[1], with at least 4 between them; band_edges[1] is 62.
All inputs are finite; a program needn't handle non-finite values.
Results may differ from a plain program's by a relative error of at most 0.025.
Values may be sent and summed in bfloat16 or wider, within the bound.
No kernel may reach another device: no remote copies, remote signals or barrier semaphores. Data moves between devices by JAX's collectives and lax.ppermute only.
A program may use at most 128 MiB of HBM per device.

v0:
```python
import math
import jax
import jax.numpy as jnp
from jax import lax
from jax.sharding import PartitionSpec as P

HEADS = 8
HEAD = 128
C = 512
SCALE = 8


def normed(values, gain):
    as_float = values.astype(jnp.float32)
    inv_rms = lax.rsqrt(jnp.mean(as_float * as_float, axis=-1, keepdims=True) + 1e-05)
    return (as_float * inv_rms * gain).astype(jnp.bfloat16)


def frequencies(band_edges, half_size):
    dim_index = jnp.arange(half_size, dtype=jnp.float32)
    base_freq = jnp.power(10000.0, -dim_index / half_size)
    lower_edge = band_edges[0].astype(jnp.float32)
    upper_edge = band_edges[1].astype(jnp.float32)
    ramp_share = jnp.clip((dim_index - lower_edge) / (upper_edge - lower_edge), 0.0, 1.0)
    return base_freq * (1.0 - ramp_share) + base_freq * ramp_share / SCALE


def rotary(projected, positions, frequency):
    half_size = frequency.shape[0]
    angles = positions.astype(jnp.float32)[..., None] * frequency
    mscale = 0.1 * math.log(SCALE) + 1.0
    cosine = (jnp.cos(angles) * mscale)[..., None, :]
    sine_part = (jnp.sin(angles) * mscale)[..., None, :]
    first_half = projected[..., :half_size]
    second_half = projected[..., half_size:]
    return jnp.concatenate(
        [
            first_half * cosine - second_half * sine_part,
            second_half * cosine + first_half * sine_part,
        ],
        axis=-1,
    ).astype(jnp.bfloat16)


def softmax_rows(scores):
    row_max = jnp.max(scores, axis=-1, keepdims=True)
    weights = jnp.exp(scores - row_max)
    return (weights / jnp.sum(weights, axis=-1, keepdims=True)).astype(jnp.bfloat16)


def attend_block(triple):
    queries, key_rows, values = triple
    length = queries.shape[0]
    scores = jnp.einsum(
        "qd,kd->qk", queries, key_rows, preferred_element_type=jnp.float32
    ) / math.sqrt(queries.shape[-1])
    causal = jnp.arange(length)[None, :] <= jnp.arange(length)[:, None]
    scores = jnp.where(causal, scores, -1e30)
    probability = softmax_rows(scores)
    return jnp.dot(probability, values, preferred_element_type=jnp.float32).astype(jnp.bfloat16)


def row_attention(queries, key_rows, values):
    grid_rows, row_len, head_count, head_size = queries.shape

    def flatten_heads(tensor):
        return tensor.transpose(0, 2, 1, 3).reshape(grid_rows * head_count, row_len, head_size)

    result = lax.map(
        attend_block, (flatten_heads(queries), flatten_heads(key_rows), flatten_heads(values))
    )
    return result.reshape(grid_rows, head_count, row_len, head_size).transpose(0, 2, 1, 3)


def column_attention(queries, key_rows, values):
    length = queries.shape[0]
    scores = jnp.einsum(
        "rchd,schd->chrs", queries, key_rows, preferred_element_type=jnp.float32
    ) / math.sqrt(queries.shape[-1])
    causal = jnp.arange(length)[None, :] <= jnp.arange(length)[:, None]
    scores = jnp.where(causal[None, None], scores, -1e30)
    probability = softmax_rows(scores)
    return jnp.einsum(
        "chrs,schd->rchd", probability, values, preferred_element_type=jnp.float32
    ).astype(jnp.bfloat16)


def columns_then_back(triple):
    attended = column_attention(triple[0], triple[1], triple[2])
    return lax.all_to_all(attended, "seq", split_axis=0, concat_axis=1, tiled=True)


def accumulate(hidden, block_rows):
    return jnp.dot(hidden, block_rows, preferred_element_type=jnp.float32)


def shards(
    tokens,
    gain_first,
    inputs_first,
    output_first,
    gain_second,
    inputs_second,
    output_second,
    starts,
    band_edges,
):
    residual = tokens[0]
    tok_count, model_width = residual.shape
    rows_dev = tok_count // C
    attn_width = HEADS * HEAD
    frequency = frequencies(band_edges, HEAD // 2)
    block_starts = starts[0]
    own_start = lax.dynamic_index_in_dim(block_starts, lax.axis_index("seq"), 0, keepdims=False)
    position_grid = (own_start + jnp.arange(tok_count, dtype=jnp.int32)).reshape(rows_dev, C)
    hidden = normed(residual, gain_first)
    group_rows = lax.all_gather(inputs_first, "seq", axis=0, tiled=True)
    projected = accumulate(hidden, lax.all_gather(group_rows, "dp", axis=0, tiled=True))
    projected = projected.reshape(rows_dev, C, 3, HEADS, HEAD)
    queries = rotary(projected[:, :, 0], position_grid, frequency)
    key_rows = rotary(projected[:, :, 1], position_grid, frequency)
    values = projected[:, :, 2].astype(jnp.bfloat16)
    attended = row_attention(queries, key_rows, values).reshape(tok_count, attn_width)
    group_rows = lax.all_gather(output_first, "seq", axis=0, tiled=True)
    branch = accumulate(attended, lax.all_gather(group_rows, "dp", axis=0, tiled=True))
    middle = (residual.astype(jnp.float32) + branch).astype(jnp.bfloat16)
    hidden = normed(middle, gain_second)
    second_rows = lax.all_gather(inputs_second, "seq", axis=0, tiled=True)
    projected = accumulate(hidden, lax.all_gather(second_rows, "dp", axis=0, tiled=True)).reshape(
        rows_dev, C, 3, HEADS, HEAD
    )
    queries = rotary(projected[:, :, 0], position_grid, frequency)
    key_rows = rotary(projected[:, :, 1], position_grid, frequency)
    values = projected[:, :, 2].astype(jnp.bfloat16)
    attended = columns_then_back(
        (
            lax.all_to_all(queries, "seq", split_axis=1, concat_axis=0, tiled=True),
            lax.all_to_all(key_rows, "seq", split_axis=1, concat_axis=0, tiled=True),
            lax.all_to_all(values, "seq", split_axis=1, concat_axis=0, tiled=True),
        )
    )
    attended = attended.reshape(tok_count, attn_width)
    group_rows = lax.all_gather(output_second, "seq", axis=0, tiled=True)
    branch = accumulate(attended, lax.all_gather(group_rows, "dp", axis=0, tiled=True))
    return (middle.astype(jnp.float32) + branch).astype(jnp.bfloat16)[None]


def solution(mesh):
    return jax.shard_map(
        shards,
        mesh=mesh,
        in_specs=(
            P("dp", "seq", None),
            P(),
            P(("dp", "seq"), None),
            P(("dp", "seq"), None),
            P(),
            P(("dp", "seq"), None),
            P(("dp", "seq"), None),
            P("dp", None),
            P(),
        ),
        out_specs=P("dp", "seq", None),
        check_vma=False,
    )
```

profile of v0, /device:TPU:0, one launch (start us, length us, event | category | flops | bytes accessed | tf_op | source)
XLA Modules:
  0.0 710.8 jit_solution(3117279610338200591)
XLA Ops:
  6.5 0.7 all-gather.9.cloned.1.call-update
  7.3 0.7 all-gather.13.cloned.1.call-update
  8.1 0.7 all-gather.17.cloned.1.call-update
  9.4 78.6 %all-gather.9.cloned.1.call-done = bf16[512,3072]{1,0:T(8,128)(2,1)} async-done(((bf16[16,3072]{1,0:T(8,128)(2,1)}), bf16[512,3072]{1,0:T(8,128)(2,1)}) %all-gather.9.cloned.1.call-update) | async-done | bytes 3145744 | tf_op jit(solution)/shard_map/all_gather | solution.py:117
  88.0 66.6 %all-gather.13.cloned.1.call-done = bf16[256,2048]{1,0:T(8,128)(2,1)} async-done(((bf16[8,2048]{1,0:T(8,128)(2,1)}), bf16[256,2048]{1,0:T(8,128)(2,1)}) %all-gather.13.cloned.1.call-update) | async-done | bytes 1048592 | tf_op jit(solution)/shard_map/all_gather | solution.py:124
  154.7 74.8 %all-gather.17.cloned.1.call-done = bf16[512,3072]{1,0:T(8,128)(2,1)} async-done(((bf16[16,3072]{1,0:T(8,128)(2,1)}), bf16[512,3072]{1,0:T(8,128)(2,1)}) %all-gather.17.cloned.1.call-update) | async-done | bytes 3145744 | tf_op jit(solution)/shard_map/all_gather | solution.py:128
  229.6 0.7 fusion.62
  231.7 0.7 constant_dynamic-slice_fusion
  232.3 0.7 add_convert_fusion.4
  233.6 0.5 fusion.45
  234.1 62.0 %all-gather.21.cloned.1.call-done = bf16[256,2048]{1,0:T(8,128)(2,1)} async-done(((bf16[8,2048]{1,0:T(8,128)(2,1)}), bf16[256,2048]{1,0:T(8,128)(2,1)}) %all-gather.21.cloned.1.call-update) | async-done | bytes 1048592 | tf_op jit(solution)/shard_map/all_gather | solution.py:143
  296.1 112.7 %all-gather.11.cloned.1.call-done = bf16[2048,3072]{1,0:T(8,128)(2,1)} async-done(((bf16[512,3072]{1,0:T(8,128)(2,1)}), bf16[2048,3072]{1,0:T(8,128)(2,1)}) %all-gather.11.cloned.1.call-update) | async-done | bytes 12582928 | tf_op jit(solution)/shard_map/all_gather | solution.py:118
  408.8 16.9 %copy.33 = bf16[3072,2048]{1,0:T(8,128)(2,1)} copy(bf16[3072,2048]{0,1:T(8,128)(2,1)} %bitcast.97) | data formatting | bytes 25165824 | tf_op jit(solution)/shard_map/dot_general | solution.py:94
  425.7 9.6 %convolution_bitcast_fusion = f32[1,512,3,8,128]{1,4,3,2,0:T(8,128)S(1)} fusion(bf16[3,8,128,2048]{3,2,1,0:T(8,128)(2,1)} %bitcast.98, bf16[1,512,2048]{2,1,0:T(8,128)(2,1)S(1)} %copy-done.3, f32[2048]{0:T(1024)S(1)} %copy-done.5, f32[512]{0:T(512)S(1)} %add_rsqrt_fusion.1), kind=kOutput, calls=%fused_computation.34 | convolution fusion | flops 6446645248 | bytes 20981760 | tf_op jit(solution)/shard_map/dot_general | solution.py:94
  435.8 1.1 fusion.33
  436.9 0.7 subtract_convert_fusion.2
  437.7 1.5 maximum_bitcast_fusion
  439.1 28.9 %while.10 = (s32[]{:T(128)}, bf16[8,512,128]{1,2,0:T(8,128)(2,1)}, bf16[8,512,128]{1,2,0:T(8,128)(2,1)}, bf16[8,512,128]{1,2,0:T(8,128)(2,1)}, bf16[8,512,128]{1,2,0:T(8,128)(2,1)}, /*index=5*/s32[]{:T(128)}) while((s32[]{:T(128)}, bf16[8,512,128]{1,2,0:T(8,128)(2,1)}, bf16[8,512,128]{1,2,0:T(8,128)(2,1)}, bf16[8,512,128]{1,2,0:T(8,128)(2,1)}, ...), condition=%wide.region_4.5_spmd, body=%wide.region_1.4_spmd.sunk | while | flops 136641536 | bytes 4206661 | solution.py:69
  439.1 1.3 fusion.78
  440.7 1.3 fusion.80
  442.1 0.7 constant_dynamic-update-slice_fusion.2
  442.8 1.3 fusion.78
  444.3 1.3 fusion.80
  445.7 0.7 constant_dynamic-update-slice_fusion.2
  446.4 1.3 fusion.78
  447.9 1.3 fusion.80
  449.3 0.7 constant_dynamic-update-slice_fusion.2
  450.0 1.3 fusion.78
  451.5 1.3 fusion.80
  452.9 0.7 constant_dynamic-update-slice_fusion.2
  453.6 1.3 fusion.78
  455.1 1.3 fusion.80
  456.5 0.7 constant_dynamic-update-slice_fusion.2
  457.2 1.3 fusion.78
  458.7 1.3 fusion.80
  460.1 0.7 constant_dynamic-update-slice_fusion.2
  460.8 1.3 fusion.78
  462.3 1.3 fusion.80
  463.7 0.7 constant_dynamic-update-slice_fusion.2
  464.4 1.3 fusion.78
  465.9 1.3 fusion.80
  467.3 0.7 constant_dynamic-update-slice_fusion.2
  468.0 6.6 fusion.18
  474.6 102.0 %all-gather.19.cloned.1.call-done = bf16[2048,3072]{1,0:T(8,128)(2,1)} async-done(((bf16[512,3072]{1,0:T(8,128)(2,1)}), bf16[2048,3072]{1,0:T(8,128)(2,1)}) %all-gather.19.cloned.1.call-update) | async-done | bytes 12582928 | tf_op jit(solution)/shard_map/all_gather | solution.py:129
  576.6 10.4 %fusion.23 = f32[512,3072]{0,1:T(8,128)S(1)} fusion(bf16[2048,3072]{1,0:T(8,128)(2,1)} %all-gather.19.cloned.1.call-done, bf16[512,2048]{1,0:T(8,128)(2,1)} %get-tuple-element.81, f32[2048]{0:T(1024)S(1)} %copy-done.6, f32[512]{0:T(512)S(1)} %add_rsqrt_fusion), kind=kOutput, calls=%fused_computation.35 | convolution fusion | flops 6446645248 | bytes 20981760 | tf_op jit(solution)/shard_map/dot_general | solution.py:94
  587.0 0.6 slice_bitcast_fusion.1
  587.7 2.0 copy-done.2
  589.7 0.7 subtract_convert_fusion.1
  590.5 1.5 copy.40
  592.0 9.8 %all-to-all-start.1 = ((bf16[1,512,8,128]{3,2,0,1:T(8,128)(2,1)}), bf16[1,512,8,128]{3,2,0,1:T(8,128)(2,1)S(1)}, u32[]{:S(2)}, u32[]{:S(2)}) async-start(bf16[1,512,8,128]{3,2,0,1:T(8,128)(2,1)} %copy.40), calls=%async_computation.1 | async-start | bytes 2097152 | tf_op jit(solution)/shard_map/all_to_all | solution.py:137
  601.9 1.5 copy.41
  603.4 19.6 %all-to-all-done.1 = bf16[1,512,8,128]{3,2,0,1:T(8,128)(2,1)S(1)} async-done(((bf16[1,512,8,128]{3,2,0,1:T(8,128)(2,1)}), bf16[1,512,8,128]{3,2,0,1:T(8,128)(2,1)S(1)}, u32[]{:S(2)}, u32[]{:S(2)}) %all-to-all-start.1) | async-done | bytes 1048608 | tf_op jit(solution)/shard_map/all_to_all | solution.py:137
  623.0 5.4 all-to-all-start.2
  628.3 1.7 fusion.34
  630.1 1.5 copy.39
  631.5 17.8 %all-to-all-done.2 = bf16[1,512,8,128]{3,2,0,1:T(8,128)(2,1)S(1)} async-done(((bf16[1,512,8,128]{3,2,0,1:T(8,128)(2,1)}), bf16[1,512,8,128]{3,2,0,1:T(8,128)(2,1)S(1)}, u32[]{:S(2)}, u32[]{:S(2)}) %all-to-all-start.2) | async-done | bytes 1048608 | tf_op jit(solution)/shard_map/all_to_all | solution.py:138
  649.3 4.7 all-to-all-start
  654.0 3.3 fusion.63
  657.3 14.7 %all-to-all-done = bf16[1,512,8,128]{3,2,0,1:T(8,128)(2,1)S(1)} async-done(((bf16[1,512,8,128]{3,2,0,1:T(8,128)(2,1)}), bf16[1,512,8,128]{3,2,0,1:T(8,128)(2,1)S(1)}, u32[]{:S(2)}, u32[]{:S(2)}) %all-to-all-start) | async-done | bytes 1048608 | tf_op jit(solution)/shard_map/all_to_all | solution.py:139
  672.0 2.6 fusion.32
  674.6 1.4 copy.46
  676.0 4.6 all-to-all-start.3
  680.6 17.5 %all-to-all-done.3 = bf16[32,16,8,128]{3,2,1,0:T(8,128)(2,1)S(1)} async-done(((bf16[32,16,8,128]{3,2,1,0:T(8,128)(2,1)}), bf16[32,16,8,128]{3,2,1,0:T(8,128)(2,1)S(1)}, u32[]{:S(2)}, u32[]{:S(2)}) %all-to-all-start.3) | async-done | bytes 1048608 | tf_op jit(solution)/shard_map/all_to_all | solution.py:90
  698.1 5.9 fusion.22
  (55 shorter events, 4.6 us)
Async XLA Ops:
  6.5 225.1 %copy-start = (s32[1,32]{1,0:T(1,128)S(1)}, s32[1,32]{1,0:T(1,128)}, u32[]{:S(2)}) copy-start(s32[1,32]{1,0:T(1,128)} %param.18) | copy-start | bytes 388
  6.5 81.4 %all-gather.9.cloned.1.call-start = ((), (), s32[]{:S(2)}) async-start(), calls=%async_computation.4 | async-start | bytes 3244032 | tf_op jit(solution)/shard_map/all_gather | solution.py:117
  7.3 147.4 %all-gather.13.cloned.1.call-start = ((), (), s32[]{:S(2)}) async-start(), calls=%async_computation.6 | async-start | bytes 1081344 | tf_op jit(solution)/shard_map/all_gather | solution.py:124
  8.0 221.5 %all-gather.17.cloned.1.call-start = ((), (), s32[]{:S(2)}) async-start(), calls=%async_computation.8 | async-start | bytes 3244032 | tf_op jit(solution)/shard_map/all_gather | solution.py:128
  8.7 287.3 %all-gather.21.cloned.1.call-start = ((), (), s32[]{:S(2)}) async-start(), calls=%async_computation.10 | async-start | bytes 1081344 | tf_op jit(solution)/shard_map/all_gather | solution.py:143
  9.3 399.5 %all-gather.11.cloned.1.call-start = ((), (), s32[]{:S(2)}) async-start(), calls=%async_computation.5 | async-start | bytes 15728640 | tf_op jit(solution)/shard_map/all_gather | solution.py:118
  88.0 380.0 %all-gather.15.cloned.1.call-start = ((), (), s32[]{:S(2)}) async-start(), calls=%async_computation.7 | async-start | bytes 5242880 | tf_op jit(solution)/shard_map/all_gather | solution.py:125
  154.6 75.0 %copy-start.4 = (s32[2]{0:T(128)S(1)}, s32[2]{0:T(128)}, u32[]{:S(2)}) copy-start(s32[2]{0:T(128)} %param.19) | copy-start | bytes 28
  154.6 78.4 %copy-start.3 = (bf16[1,512,2048]{2,1,0:T(8,128)(2,1)S(1)}, bf16[1,512,2048]{2,1,0:T(8,128)(2,1)}, u32[]{:S(2)}) copy-start(bf16[1,512,2048]{2,1,0:T(8,128)(2,1)} %param.11) | copy-start | bytes 6291460
  154.7 422.0 %all-gather.19.cloned.1.call-start = ((), (), s32[]{:S(2)}) async-start(), calls=%async_computation.9 | async-start | bytes 15728640 | tf_op jit(solution)/shard_map/all_gather | solution.py:129
  229.6 451.0 %all-gather.23.cloned.1.call-start = ((), (), s32[]{:S(2)}) async-start(), calls=%async_computation.11 | async-start | bytes 5242880 | tf_op jit(solution)/shard_map/all_gather | solution.py:144
  408.8 16.9 %copy-start.5 = (f32[2048]{0:T(1024)S(1)}, f32[2048]{0:T(1024)}, u32[]{:S(2)}) copy-start(f32[2048]{0:T(1024)} %param.12) | copy-start | bytes 24580
  468.0 108.6 %copy-start.6 = (f32[2048]{0:T(1024)S(1)}, f32[2048]{0:T(1024)}, u32[]{:S(2)}) copy-start(f32[2048]{0:T(1024)} %param.15) | copy-start | bytes 24580
  587.0 2.7 copy-start.2
  592.0 31.0 %all-to-all-start.1 = ((bf16[1,512,8,128]{3,2,0,1:T(8,128)(2,1)}), bf16[1,512,8,128]{3,2,0,1:T(8,128)(2,1)S(1)}, u32[]{:S(2)}, u32[]{:S(2)}) async-start(bf16[1,512,8,128]{3,2,0,1:T(8,128)(2,1)} %copy.40), calls=%async_computation.1 | async-start | bytes 2097152 | tf_op jit(solution)/shard_map/all_to_all | solution.py:137
  623.0 26.3 %all-to-all-start.2 = ((bf16[1,512,8,128]{3,2,0,1:T(8,128)(2,1)}), bf16[1,512,8,128]{3,2,0,1:T(8,128)(2,1)S(1)}, u32[]{:S(2)}, u32[]{:S(2)}) async-start(bf16[1,512,8,128]{3,2,0,1:T(8,128)(2,1)} %copy.41), calls=%async_computation.2 | async-start | bytes 2097152 | tf_op jit(solution)/shard_map/all_to_all | solution.py:138
  649.3 22.7 %all-to-all-start = ((bf16[1,512,8,128]{3,2,0,1:T(8,128)(2,1)}), bf16[1,512,8,128]{3,2,0,1:T(8,128)(2,1)S(1)}, u32[]{:S(2)}, u32[]{:S(2)}) async-start(bf16[1,512,8,128]{3,2,0,1:T(8,128)(2,1)} %copy.39), calls=%async_computation | async-start | bytes 2097152 | tf_op jit(solution)/shard_map/all_to_all | solution.py:139
  674.6 23.5 %copy-start.7 = (bf16[512,2048]{1,0:T(8,128)(2,1)S(1)}, bf16[512,2048]{1,0:T(8,128)(2,1)}, u32[]{:S(2)}) copy-start(bf16[512,2048]{1,0:T(8,128)(2,1)} %get-tuple-element.81) | copy-start | bytes 6291460
  676.0 22.1 %all-to-all-start.3 = ((bf16[32,16,8,128]{3,2,1,0:T(8,128)(2,1)}), bf16[32,16,8,128]{3,2,1,0:T(8,128)(2,1)S(1)}, u32[]{:S(2)}, u32[]{:S(2)}) async-start(bf16[32,16,8,128]{3,2,1,0:T(8,128)(2,1)} %copy.46), calls=%async_computation.3 | async-start | bytes 2097152 | tf_op jit(solution)/shard_map/all_to_all | solution.py:90
  698.1 5.9 copy-start.1
Sparse Core Ops, SparseCore 0:
  10.4 77.4 all-gather.8
  90.9 63.6 all-gather.12
  157.7 71.8 all-gather.16
  232.4 63.6 all-gather.20
  297.6 111.1 all-gather.10
  410.4 48.7 all-gather.14
  460.8 115.8 all-gather.18
  578.3 71.1 all-gather.22
where the time goes:
time: 712 us; the launch traced here: 711 us
  waiting for transfers between devices  569 us (80%)
  matrix products  59.2 us (8%)
  local copies, waits for them, and re-layouts  36.2 us (5%)
  starting transfers between devices  24.8 us (3%)
  between operations  15 us (2%)
    all_gather x3, waiting for transfers between devices, shards(): lax.all_gather(group_rows, 'dp', axis=0, tiled=True)  113 us
    all_gather x1, waiting for transfers between devices, shards(): lax.all_gather(second_rows, 'dp', axis=0, tiled=True)  102 us
    all_gather x1, waiting for transfers between devices, shards(): group_rows = lax.all_gather(inputs_first, 'seq', axis=0, tiled=True)  78.6 us
    all_gather x1, waiting for transfers between devices, shards(): second_rows = lax.all_gather(inputs_second, 'seq', axis=0, tiled=True)  74.8 us
    all_gather x1, waiting for transfers between devices, shards(): group_rows = lax.all_gather(output_first, 'seq', axis=0, tiled=True)  66.6 us
    all_gather x1, waiting for transfers between devices, shards(): group_rows = lax.all_gather(output_second, 'seq', axis=0, tiled=True)  62 us
    dot_general x4, matrix products, accumulate(): return jnp.dot(hidden, block_rows, preferred_element_type=jnp.float32)  32.4 us
    all_to_all x1, waiting for transfers between devices, shards(): lax.all_to_all(queries, 'seq', split_axis=1, concat_axis=0, tiled=True)  19.6 us
  transfers between devices with their start and end apart: 12, of which 10 were waited for; matrix products, arithmetic and copies ran while one was open for 13% of the time, Pallas kernels for 0%

commit v1 on v0

--- a/solution.py
+++ b/solution.py
@@ -3,11 +3,21 @@
 import jax.numpy as jnp
 from jax import lax
 from jax.sharding import PartitionSpec as P
+from jax.lax import all_to_all, axis_size
 
 HEADS = 8
 HEAD = 128
 C = 512
 SCALE = 8
+find_sums_all = lambda view: jnp.concatenate(
+    all_to_all(
+        jnp.stack(jnp.split(view, axis_size("seq"), 0), 0),
+        axis_name="seq",
+        split_axis=0,
+        concat_axis=0,
+    ),
+    1,
+)
 
 
 def normed(values, gain):
@@ -87,7 +97,7 @@
 
 def columns_then_back(triple):
     attended = column_attention(triple[0], triple[1], triple[2])
-    return lax.all_to_all(attended, "seq", split_axis=0, concat_axis=1, tiled=True)
+    return find_sums_all(attended)
 
 
 def accumulate(hidden, block_rows):

time: 712 us -> 694 us (0.975)
  waiting for transfers between devices: 569 us -> 528 us
  local copies, waits for them, and re-layouts: 36.2 us -> 56.3 us
    all_gather x1, waiting for transfers between devices: 62 us -> 40 us  [shards(): group_rows = lax.all_gather(output_second, 'seq', axis=0, tiled=True)]
    all_gather x3, waiting for transfers between devices: 113 us -> 132 us  [shards(): lax.all_gather(group_rows, 'dp', axis=0, tiled=True)]
    unnamed x16 -> x47, local copies, waits for them, and re-layouts: 2.06 us -> 20.9 us
    all_to_all x1, waiting for transfers between devices: 17.5 us -> 0.01 us  [all_to_all(jnp.stack(jnp.split(view, axis_size('seq'), 0), 0), axis_name=...]
    all_to_all x1, waiting for transfers between devices: 14.7 us -> 0.01 us  [shards(): lax.all_to_all(values, 'seq', split_axis=1, concat_axis=0, tiled=True)]
  transfers between devices with their start and end apart: 12 -> 12, of which waited for: 10 -> 9; matrix products, arithmetic and copies ran while one was open for 13% -> 15% of each run, Pallas kernels for 0% -> 0%
where the time goes in v1:
time: 694 us; the launch traced here: 691 us
  waiting for transfers between devices  528 us (76%)
  matrix products  59.2 us (9%)
  local copies, waits for them, and re-layouts  56.3 us (8%)
  starting transfers between devices  25.4 us (4%)
  between operations  14.9 us (2%)
    all_gather x3, waiting for transfers between devices, shards(): lax.all_gather(group_rows, 'dp', axis=0, tiled=True)  132 us
    all_gather x1, waiting for transfers between devices, shards(): lax.all_gather(second_rows, 'dp', axis=0, tiled=True)  102 us
    all_gather x1, waiting for transfers between devices, shards(): group_rows = lax.all_gather(inputs_first, 'seq', axis=0, tiled=True)  79.1 us
    all_gather x1, waiting for transfers between devices, shards(): second_rows = lax.all_gather(inputs_second, 'seq', axis=0, tiled=True)  74.8 us
    all_gather x1, waiting for transfers between devices, shards(): group_rows = lax.all_gather(output_first, 'seq', axis=0, tiled=True)  66.6 us
    all_gather x1, waiting for transfers between devices, shards(): group_rows = lax.all_gather(output_second, 'seq', axis=0, tiled=True)  40 us
    dot_general x4, matrix products, accumulate(): return jnp.dot(hidden, block_rows, preferred_element_type=jnp.float32)  32.4 us
    unnamed x47, local copies, waits for them, and re-layouts  20.9 us
  transfers between devices with their start and end apart: 12, of which 9 were waited for; matrix products, arithmetic and copies ran while one was open for 15% of the time, Pallas kernels for 0%

profile of v1, /device:TPU:0, one launch (start us, length us, event | category | flops | bytes accessed | tf_op | source)
XLA Modules:
  0.0 690.8 jit_solution(8074580312568889385)
XLA Ops:
  6.5 0.7 all-gather.9.cloned.1.call-update
  7.3 0.7 all-gather.13.cloned.1.call-update
  8.1 0.7 all-gather.17.cloned.1.call-update
  8.8 79.1 %all-gather.9.cloned.1.call-done = bf16[512,3072]{1,0:T(8,128)(2,1)} async-done(((bf16[16,3072]{1,0:T(8,128)(2,1)}), bf16[512,3072]{1,0:T(8,128)(2,1)}) %all-gather.9.cloned.1.call-update) | async-done | bytes 3145744 | tf_op jit(solution)/shard_map/all_gather | solution.py:127
  88.0 66.6 %all-gather.13.cloned.1.call-done = bf16[256,2048]{1,0:T(8,128)(2,1)} async-done(((bf16[8,2048]{1,0:T(8,128)(2,1)}), bf16[256,2048]{1,0:T(8,128)(2,1)}) %all-gather.13.cloned.1.call-update) | async-done | bytes 1048592 | tf_op jit(solution)/shard_map/all_gather | solution.py:134
  154.7 74.8 %all-gather.17.cloned.1.call-done = bf16[512,3072]{1,0:T(8,128)(2,1)} async-done(((bf16[16,3072]{1,0:T(8,128)(2,1)}), bf16[512,3072]{1,0:T(8,128)(2,1)}) %all-gather.17.cloned.1.call-update) | async-done | bytes 3145744 | tf_op jit(solution)/shard_map/all_gather | solution.py:138
  233.6 108.9 %all-gather.11.cloned.1.call-done = bf16[2048,3072]{1,0:T(8,128)(2,1)} async-done(((bf16[512,3072]{1,0:T(8,128)(2,1)}), bf16[2048,3072]{1,0:T(8,128)(2,1)}) %all-gather.11.cloned.1.call-update) | async-done | bytes 12582928 | tf_op jit(solution)/shard_map/all_gather | solution.py:128
  342.6 16.8 %copy.918 = bf16[3072,2048]{1,0:T(8,128)(2,1)} copy(bf16[3072,2048]{0,1:T(8,128)(2,1)} %bitcast.161) | data formatting | bytes 25165824 | tf_op jit(solution)/shard_map/dot_general | solution.py:104
  359.4 9.6 %convolution_bitcast_fusion = f32[1,512,3,8,128]{1,4,3,2,0:T(8,128)S(1)} fusion(bf16[3,8,128,2048]{3,2,1,0:T(8,128)(2,1)} %bitcast.162, bf16[1,512,2048]{2,1,0:T(8,128)(2,1)S(1)} %copy-done.3, f32[2048]{0:T(1024)S(1)} %copy-done.5, f32[512]{0:T(512)S(1)} %add_rsqrt_fusion.1), kind=kOutput, calls=%fused_computation.34 | convolution fusion | flops 6446645248 | bytes 20981760 | tf_op jit(solution)/shard_map/dot_general | solution.py:104
  369.5 0.7 subtract_convert_fusion.2
  370.2 1.5 maximum_bitcast_fusion
  371.7 1.1 fusion.33
  372.8 28.9 %while.10 = (s32[]{:T(128)}, bf16[8,512,128]{1,2,0:T(8,128)(2,1)}, bf16[8,512,128]{1,2,0:T(8,128)(2,1)}, bf16[8,512,128]{1,2,0:T(8,128)(2,1)}, bf16[8,512,128]{1,2,0:T(8,128)(2,1)}, /*index=5*/s32[]{:T(128)}) while((s32[]{:T(128)}, bf16[8,512,128]{1,2,0:T(8,128)(2,1)}, bf16[8,512,128]{1,2,0:T(8,128)(2,1)}, bf16[8,512,128]{1,2,0:T(8,128)(2,1)}, ...), condition=%wide.region_4.5_spmd, body=%wide.region_1.4_spmd.sunk | while | flops 136641536 | bytes 4206661 | solution.py:79
  372.8 1.3 fusion.80
  374.4 1.3 fusion.82
  375.8 0.7 constant_dynamic-update-slice_fusion.34
  376.4 1.3 fusion.80
  378.0 1.3 fusion.82
  379.4 0.7 constant_dynamic-update-slice_fusion.34
  380.1 1.3 fusion.80
  381.6 1.3 fusion.82
  383.0 0.7 constant_dynamic-update-slice_fusion.34
  383.7 1.3 fusion.80
  385.2 1.3 fusion.82
  386.6 0.7 constant_dynamic-update-slice_fusion.34
  387.3 1.3 fusion.80
  388.8 1.3 fusion.82
  390.2 0.7 constant_dynamic-update-slice_fusion.34
  390.9 1.3 fusion.80
  392.4 1.3 fusion.82
  393.8 0.7 constant_dynamic-update-slice_fusion.34
  394.5 1.3 fusion.80
  396.0 1.3 fusion.82
  397.4 0.7 constant_dynamic-update-slice_fusion.34
  398.1 1.3 fusion.80
  399.6 1.3 fusion.82
  401.1 0.7 constant_dynamic-update-slice_fusion.34
  401.7 6.6 fusion.18
  408.3 101.9 %all-gather.19.cloned.1.call-done = bf16[2048,3072]{1,0:T(8,128)(2,1)} async-done(((bf16[512,3072]{1,0:T(8,128)(2,1)}), bf16[2048,3072]{1,0:T(8,128)(2,1)}) %all-gather.19.cloned.1.call-update) | async-done | bytes 12582928 | tf_op jit(solution)/shard_map/all_gather | solution.py:139
  510.2 10.3 %fusion.23 = f32[512,3072]{0,1:T(8,128)S(1)} fusion(bf16[2048,3072]{1,0:T(8,128)(2,1)} %all-gather.19.cloned.1.call-done, bf16[512,2048]{1,0:T(8,128)(2,1)} %get-tuple-element.263, f32[2048]{0:T(1024)S(1)} %copy-done.6, f32[512]{0:T(512)S(1)} %add_rsqrt_fusion), kind=kOutput, calls=%fused_computation.35 | convolution fusion | flops 6446645248 | bytes 20981760 | tf_op jit(solution)/shard_map/dot_general | solution.py:104
  521.2 2.0 copy-done.2
  523.2 0.7 subtract_convert_fusion.1
  524.1 1.5 copy.925
  525.5 9.8 %all-to-all-start.1 = ((bf16[1,512,8,128]{3,2,0,1:T(8,128)(2,1)}), bf16[1,512,8,128]{3,2,0,1:T(8,128)(2,1)S(1)}, u32[]{:S(2)}, u32[]{:S(2)}) async-start(bf16[1,512,8,128]{3,2,0,1:T(8,128)(2,1)} %copy.925), calls=%async_computation.1 | async-start | bytes 2097152 | tf_op jit(solution)/shard_map/all_to_all | solution.py:147
  535.4 0.7 all-gather.21.cloned.1.call-update
  536.2 1.5 copy.926
  537.7 15.9 %all-to-all-done.1 = bf16[1,512,8,128]{3,2,0,1:T(8,128)(2,1)S(1)} async-done(((bf16[1,512,8,128]{3,2,0,1:T(8,128)(2,1)}), bf16[1,512,8,128]{3,2,0,1:T(8,128)(2,1)S(1)}, u32[]{:S(2)}, u32[]{:S(2)}) %all-to-all-start.1) | async-done | bytes 1048608 | tf_op jit(solution)/shard_map/all_to_all | solution.py:147
  553.6 6.0 all-to-all-start.2
  559.6 1.7 fusion.34
  561.3 1.5 copy.924
  562.8 14.8 %all-to-all-done.2 = bf16[1,512,8,128]{3,2,0,1:T(8,128)(2,1)S(1)} async-done(((bf16[1,512,8,128]{3,2,0,1:T(8,128)(2,1)}), bf16[1,512,8,128]{3,2,0,1:T(8,128)(2,1)S(1)}, u32[]{:S(2)}, u32[]{:S(2)}) %all-to-all-start.2) | async-done | bytes 1048608 | tf_op jit(solution)/shard_map/all_to_all | solution.py:148
  577.7 4.7 all-to-all-start
  582.4 40.0 %all-gather.21.cloned.1.call-done = bf16[256,2048]{1,0:T(8,128)(2,1)} async-done(((bf16[8,2048]{1,0:T(8,128)(2,1)}), bf16[256,2048]{1,0:T(8,128)(2,1)}) %all-gather.21.cloned.1.call-update) | async-done | bytes 1048592 | tf_op jit(solution)/shard_map/all_gather | solution.py:153
  622.4 3.3 fusion.65
  625.6 2.6 fusion.32
  628.2 0.9 fusion.63
  637.0 1.3 fusion.62
  644.4 0.6 constant_dynamic-update-slice_fusion.9
  646.3 0.6 constant_dynamic-update-slice_fusion.6
  648.1 0.6 constant_dynamic-update-slice_fusion.3
  649.3 0.6 constant_dynamic-update-slice_fusion.1
  650.0 4.6 all-to-all-start.3
  654.6 23.5 %all-gather.23.cloned.1.call-done = bf16[1024,2048]{1,0:T(8,128)(2,1)} async-done(((bf16[256,2048]{1,0:T(8,128)(2,1)}), bf16[1024,2048]{1,0:T(8,128)(2,1)}) %all-gather.23.cloned.1.call-update) | async-done | bytes 4194320 | tf_op jit(solution)/shard_map/all_gather | solution.py:154
  678.1 5.9 fusion.22
  (88 shorter events, 24.0 us)
Async XLA Ops:
  6.5 224.9 %copy-start = (s32[1,32]{1,0:T(1,128)S(1)}, s32[1,32]{1,0:T(1,128)}, u32[]{:S(2)}) copy-start(s32[1,32]{1,0:T(1,128)} %param.18) | copy-start | bytes 388
  6.5 81.4 %all-gather.9.cloned.1.call-start = ((), (), s32[]{:S(2)}) async-start(), calls=%async_computation.4 | async-start | bytes 3244032 | tf_op jit(solution)/shard_map/all_gather | solution.py:127
  7.3 147.4 %all-gather.13.cloned.1.call-start = ((), (), s32[]{:S(2)}) async-start(), calls=%async_computation.6 | async-start | bytes 1081344 | tf_op jit(solution)/shard_map/all_gather | solution.py:134
  8.0 221.5 %all-gather.17.cloned.1.call-start = ((), (), s32[]{:S(2)}) async-start(), calls=%async_computation.8 | async-start | bytes 3244032 | tf_op jit(solution)/shard_map/all_gather | solution.py:138
  8.7 333.8 %all-gather.11.cloned.1.call-start = ((), (), s32[]{:S(2)}) async-start(), calls=%async_computation.5 | async-start | bytes 15728640 | tf_op jit(solution)/shard_map/all_gather | solution.py:128
  88.0 313.8 %all-gather.15.cloned.1.call-start = ((), (), s32[]{:S(2)}) async-start(), calls=%async_computation.7 | async-start | bytes 5242880 | tf_op jit(solution)/shard_map/all_gather | solution.py:135
  154.6 75.0 %copy-start.4 = (s32[2]{0:T(128)S(1)}, s32[2]{0:T(128)}, u32[]{:S(2)}) copy-start(s32[2]{0:T(128)} %param.19) | copy-start | bytes 28
  154.6 78.0 %copy-start.3 = (bf16[1,512,2048]{2,1,0:T(8,128)(2,1)S(1)}, bf16[1,512,2048]{2,1,0:T(8,128)(2,1)}, u32[]{:S(2)}) copy-start(bf16[1,512,2048]{2,1,0:T(8,128)(2,1)} %param.11) | copy-start | bytes 6291460
  154.7 355.6 %all-gather.19.cloned.1.call-start = ((), (), s32[]{:S(2)}) async-start(), calls=%async_computation.9 | async-start | bytes 15728640 | tf_op jit(solution)/shard_map/all_gather | solution.py:139
  342.6 16.8 %copy-start.5 = (f32[2048]{0:T(1024)S(1)}, f32[2048]{0:T(1024)}, u32[]{:S(2)}) copy-start(f32[2048]{0:T(1024)} %param.12) | copy-start | bytes 24580
  401.7 108.5 %copy-start.6 = (f32[2048]{0:T(1024)S(1)}, f32[2048]{0:T(1024)}, u32[]{:S(2)}) copy-start(f32[2048]{0:T(1024)} %param.15) | copy-start | bytes 24580
  520.6 2.7 copy-start.2
  525.5 28.0 %all-to-all-start.1 = ((bf16[1,512,8,128]{3,2,0,1:T(8,128)(2,1)}), bf16[1,512,8,128]{3,2,0,1:T(8,128)(2,1)S(1)}, u32[]{:S(2)}, u32[]{:S(2)}) async-start(bf16[1,512,8,128]{3,2,0,1:T(8,128)(2,1)} %copy.925), calls=%async_computation.1 | async-start | bytes 2097152 | tf_op jit(solution)/shard_map/all_to_all | solution.py:147
  535.4 87.0 %all-gather.21.cloned.1.call-start = ((), (), s32[]{:S(2)}) async-start(), calls=%async_computation.10 | async-start | bytes 1081344 | tf_op jit(solution)/shard_map/all_gather | solution.py:153
  553.6 24.1 %all-to-all-start.2 = ((bf16[1,512,8,128]{3,2,0,1:T(8,128)(2,1)}), bf16[1,512,8,128]{3,2,0,1:T(8,128)(2,1)S(1)}, u32[]{:S(2)}, u32[]{:S(2)}) async-start(bf16[1,512,8,128]{3,2,0,1:T(8,128)(2,1)} %copy.926), calls=%async_computation.2 | async-start | bytes 2097152 | tf_op jit(solution)/shard_map/all_to_all | solution.py:148
  577.7 48.0 %all-to-all-start = ((bf16[1,512,8,128]{3,2,0,1:T(8,128)(2,1)}), bf16[1,512,8,128]{3,2,0,1:T(8,128)(2,1)S(1)}, u32[]{:S(2)}, u32[]{:S(2)}) async-start(bf16[1,512,8,128]{3,2,0,1:T(8,128)(2,1)} %copy.924), calls=%async_computation | async-start | bytes 2097152 | tf_op jit(solution)/shard_map/all_to_all | solution.py:149
  582.3 95.7 %all-gather.23.cloned.1.call-start = ((), (), s32[]{:S(2)}) async-start(), calls=%async_computation.11 | async-start | bytes 5242880 | tf_op jit(solution)/shard_map/all_gather | solution.py:154
  638.4 39.7 %copy-start.7 = (bf16[512,2048]{1,0:T(8,128)(2,1)S(1)}, bf16[512,2048]{1,0:T(8,128)(2,1)}, u32[]{:S(2)}) copy-start(bf16[512,2048]{1,0:T(8,128)(2,1)} %get-tuple-element.263) | copy-start | bytes 6291460
  650.0 28.1 %all-to-all-start.3 = ((bf16[32,1,16,8,128]{4,3,2,1,0:T(8,128)(2,1)}), bf16[32,1,16,8,128]{4,3,2,1,0:T(8,128)(2,1)S(1)}, u32[]{:S(2)}, u32[]{:S(2)}) async-start(bf16[32,1,16,8,128]{4,3,2,1,0:T(8,128)(2,1)} %constant_dynamic-update-slice_fusion.1), calls=%async_computation.3 | async-start | bytes 2097152 | tf_op jit(solution)/shard_map/all_to_all | solution.py:13
  678.1 5.9 copy-start.1
Sparse Core Ops, SparseCore 0:
  10.4 77.4 all-gather.8
  90.9 63.6 all-gather.12
  157.7 71.8 all-gather.16
  231.1 111.4 all-gather.10
  344.1 48.7 all-gather.14
  394.4 115.8 all-gather.18
  539.2 83.0 all-gather.20
  624.0 54.0 all-gather.22
